TPU v7x, 32 devices: a whole 2x2x4 slice. The times are simulated.
32 devices in a mesh: clip: 8 (over z, x), tm: 4 (over y, core).
Axes of the slice: x: 2, y: 2, z: 4, core: 2. Of those that a mesh axis runs over, the one named last changes fastest.
Arguments:
- features: bfloat16 [16, 1024, 512], P('clip', 'tm'), may hold values from -6 to 6
- cotangent: bfloat16 [16, 1024, 512], P('clip', 'tm'), may hold values from -6 to 6
- clip_lengths: int32 [16], P('clip'), may hold values from 128 to 1024, as said below
- code_ids: int32 [4, 16, 1024], P(None, 'clip', 'tm'), may hold values from 0 to 1023
- step_count: int32 [1], replicated, may hold values from 2 to 20
- dilated_kernel_weight: float32 [3, 512, 256], P(None, None, 'clip'), may hold values from -0.15625 to 0.15625
- pointwise_conv: float32 [256, 512], P(None, 'clip'), may hold values from -0.75 to 0.75
- codebooks: float32 [4, 1024, 256], P(None, 'clip'), may hold values from -6 to 6
- dilated_first_moment: float32 [3, 512, 256], P(None, None, 'clip'), may hold values from -1 to 1
- dilated_second_moment: float32 [3, 512, 256], P(None, None, 'clip'), may hold values from 0.028995216 to 0.11598086
- pointwise_first: float32 [256, 512], P(None, 'clip'), may hold values from -1 to 1
- pointwise_second: float32 [256, 512], P(None, 'clip'), may hold values from 0.028995216 to 0.11598086
- codebook_first: float32 [4, 1024, 256], P(None, 'clip'), may hold values from -0.01953125 to 0.01953125
- codebook_second: float32 [4, 1024, 256], P(None, 'clip'), may hold values from 9.745614e-06 to 3.8982456e-05
Outputs:
- quantized: bfloat16 [16, 1024, 512], P('clip', 'tm')
- features_gradient: float32 [16, 1024, 512], P('clip', 'tm')
- grad_norm: float32 [1], replicated
- dilated_new: float32 [3, 512, 256], P(None, None, 'clip')
- dilated_grad: float32 [3, 512, 256], P(None, None, 'clip')
- dilated_square: float32 [3, 512, 256], P(None, None, 'clip')
- pointwise_new: float32 [256, 512], P(None, 'clip')
- pointwise_grad: float32 [256, 512], P(None, 'clip')
- pointwise_square: float32 [256, 512], P(None, 'clip')
- codebook_new: float32 [4, 1024, 256], P(None, 'clip')
- codebook_grad: float32 [4, 1024, 256], P(None, 'clip')
- codebook_square: float32 [4, 1024, 256], P(None, 'clip')
Inputs may be any that keep to these rules, and one draw needn't show every extreme that they name: `clip_lengths`: the number of valid frames of each clip; frames from it on are padding; clip 0 is always full.
All inputs are finite; a program needn't handle non-finite values.
Results may differ from a plain program's by a relative error of at most 0.001.
The roundings to bfloat16 on the way count: a program that leaves them out, or rounds other values in their place, can miss the bound.
Values may be sent and summed in bfloat16 or wider, within the bound.
No kernel may reach another device: no remote copies, remote signals or barrier semaphores. Data moves between devices by JAX's collectives and lax.ppermute only.
A program may use at most 64 MiB of HBM per device.

v0:
```python
import jax
import jax.numpy as jnp
from jax import lax
from jax.sharding import PartitionSpec as P

HID = 256
CODES = 1024
GROUPS = 2
LEVELS = 2
KERNEL = 3
DILATION = 3
DG = 256
COMMIT = 0.25
FIRST_DECAY = 0.9
SECOND_DECAY = 0.99
EPSILON = 1e-08
WEIGHT_DECAY = 0.01
BITRATE_FACTOR = 0.02
RATE_CODE = 0.5


def extended(cells, sides, width):
    for axis, dim in sides:
        count = lax.axis_size(axis)
        ends = count - 1
        head = lax.slice_in_dim(cells, 0, width, axis=dim)
        tail = lax.slice_in_dim(cells, cells.shape[dim] - width, cells.shape[dim], axis=dim)
        cells = jnp.concatenate(
            [
                lax.ppermute(tail, axis, [(i, (i + 1) % count) for i in range(ends)]),
                cells,
                lax.ppermute(head, axis, [((i + 1) % count, i) for i in range(ends)]),
            ],
            axis=dim,
        )
    return cells


def elu_slope(values):
    return jnp.where(values > 0, 1.0, jnp.exp(jnp.minimum(values, 0.0)))


def adamw_update(weight, first, second, grad, rate, completed_steps):
    first_new = FIRST_DECAY * first + (1.0 - FIRST_DECAY) * grad
    second_new = SECOND_DECAY * second + (1.0 - SECOND_DECAY) * grad * grad
    first_hat = first_new / (1.0 - FIRST_DECAY**completed_steps)
    second_hat = second_new / (1.0 - SECOND_DECAY**completed_steps)
    weight_new = weight - rate * (
        first_hat / (jnp.sqrt(second_hat) + EPSILON) + WEIGHT_DECAY * weight
    )
    return (weight_new, grad, second_new)


def shards(
    features,
    cotangent,
    clip_lengths,
    code_ids,
    step_count,
    dilated_kernel_weight,
    pointwise_conv,
    codebooks,
    dilated_first_moment,
    dilated_second_moment,
    pointwise_first,
    pointwise_second,
    codebook_first,
    codebook_second,
):
    clip_rank = lax.axis_index("clip")
    time_rank = lax.axis_index("tm")
    dilated_full, pointwise_full, table_full = (
        lax.all_gather(dilated_kernel_weight.astype(jnp.bfloat16), "clip", axis=2, tiled=True),
        lax.all_gather(pointwise_conv.astype(jnp.bfloat16), "clip", axis=1, tiled=True),
        lax.all_gather(codebooks.astype(jnp.bfloat16), "clip", axis=1, tiled=True),
    )
    clips, frames, width = features.shape
    positions = time_rank * frames + lax.broadcasted_iota(jnp.int32, (clips, frames, 1), 1)
    frame_mask = (positions < clip_lengths[:, None, None]).astype(jnp.float32)
    start = features.astype(jnp.float32) * frame_mask
    activated = jax.nn.elu(start).astype(jnp.bfloat16)
    padded = extended(activated, (("tm", 1),), DILATION)
    hidden = jnp.zeros((clips, frames, HID), jnp.float32)
    for tap_index in range(KERNEL):
        window = padded[:, tap_index * DILATION : tap_index * DILATION + frames]
        hidden = hidden + jnp.einsum(
            "btc,cd->btd", window, dilated_full[tap_index], preferred_element_type=jnp.float32
        )
    gated = jax.nn.elu(hidden).astype(jnp.bfloat16)
    latent = start + jnp.einsum(
        "btk,kd->btd", gated, pointwise_full, preferred_element_type=jnp.float32
    )
    backs = cotangent.astype(jnp.float32) * frame_mask
    latent_parts = []
    quant_parts = []
    table_grads = []
    for group in range(GROUPS):
        residual_part = latent[..., group * DG : (group + 1) * DG]
        moving_grad = backs[..., group * DG : (group + 1) * DG]
        summed = jnp.zeros_like(residual_part)
        for level in range(LEVELS):
            slot = group * LEVELS + level
            chosen = jnp.take(table_full[slot], code_ids[slot], axis=0).astype(jnp.float32)
            moving_grad = moving_grad + 2.0 * COMMIT * frame_mask * (residual_part - chosen)
            code_grad = 2.0 * frame_mask * (chosen - residual_part)
            table_grads.append(
                jax.ops.segment_sum(
                    code_grad.reshape(-1, DG), code_ids[slot].reshape(-1), num_segments=CODES
                )
            )
            residual_part = residual_part - chosen
            summed = summed + chosen
        latent_parts.append(moving_grad)
        quant_parts.append(summed)
    quantized = (jnp.concatenate(quant_parts, axis=-1) * frame_mask).astype(jnp.bfloat16)
    latent_grad = jnp.concatenate(latent_parts, axis=-1)
    table_grad = jnp.stack(table_grads, axis=0)
    branch_grad = latent_grad.astype(jnp.bfloat16)
    pointwise_grad = jnp.einsum(
        "btk,btd->kd", gated, branch_grad, preferred_element_type=jnp.float32
    )
    gated_grad = jnp.einsum(
        "btd,kd->btk", branch_grad, pointwise_full, preferred_element_type=jnp.float32
    )
    hidden_grad = (gated_grad * elu_slope(hidden)).astype(jnp.bfloat16)
    padded_grad = extended(hidden_grad, (("tm", 1),), DILATION)
    dilated_parts = []
    act_grad = jnp.zeros((clips, frames, width), jnp.float32)
    for tap_index in range(KERNEL):
        window = padded[:, tap_index * DILATION : tap_index * DILATION + frames]
        dilated_parts.append(
            jnp.einsum("btc,btd->cd", window, hidden_grad, preferred_element_type=jnp.float32)
        )
        offset = (KERNEL - 1 - tap_index) * DILATION
        act_grad = act_grad + jnp.einsum(
            "btd,cd->btc",
            padded_grad[:, offset : offset + frames],
            dilated_full[tap_index],
            preferred_element_type=jnp.float32,
        )
    dilated_grad = jnp.stack(dilated_parts, axis=0)
    features_gradient = frame_mask * (latent_grad + elu_slope(start) * act_grad)
    local_grads = (dilated_grad, pointwise_grad, table_grad)
    whole = lax.psum((local_grads[0], local_grads[1], local_grads[2]), ("clip", "tm"))
    squared = sum((jnp.sum(piece * piece) for piece in whole))
    shares = (
        lax.dynamic_slice_in_dim(
            whole[0], clip_rank * dilated_kernel_weight.shape[2], dilated_kernel_weight.shape[2], 2
        ),
        lax.dynamic_slice_in_dim(
            whole[1], clip_rank * pointwise_conv.shape[1], pointwise_conv.shape[1], 1
        ),
        lax.dynamic_slice_in_dim(whole[2], clip_rank * codebooks.shape[1], codebooks.shape[1], 1),
    )
    count = dilated_full.size + pointwise_full.size + table_full.size
    limit = jnp.sqrt(jnp.float32(count))
    gradient_norm_total = jnp.sqrt(squared)
    clip_scale_factor = limit / jnp.maximum(gradient_norm_total, limit)
    completed_steps = step_count[0].astype(jnp.float32)
    dilation_factor = adamw_update(
        dilated_kernel_weight,
        dilated_first_moment,
        dilated_second_moment,
        shares[0] * clip_scale_factor,
        BITRATE_FACTOR,
        completed_steps,
    )
    pointwise_kernel = adamw_update(
        pointwise_conv,
        pointwise_first,
        pointwise_second,
        shares[1] * clip_scale_factor,
        BITRATE_FACTOR,
        completed_steps,
    )
    codebook_tensor = adamw_update(
        codebooks,
        codebook_first,
        codebook_second,
        shares[2] * clip_scale_factor,
        RATE_CODE,
        completed_steps,
    )
    return (
        quantized,
        features_gradient,
        gradient_norm_total.reshape(1),
        dilation_factor[0],
        dilation_factor[1],
        dilation_factor[2],
        pointwise_kernel[0],
        pointwise_kernel[1],
        pointwise_kernel[2],
        codebook_tensor[0],
        codebook_tensor[1],
        codebook_tensor[2],
    )


def solution(mesh):
    in_specs = (
        P("clip", "tm", None),
        P("clip", "tm", None),
        P("clip"),
        P(None, "clip", "tm"),
        P(),
        P(None, None, "clip"),
        P(None, "clip"),
        P(None, "clip", None),
        P(None, None, "clip"),
        P(None, None, "clip"),
        P(None, "clip"),
        P(None, "clip"),
        P(None, "clip", None),
        P(None, "clip", None),
    )
    out_specs = (
        P("clip", "tm", None),
        P("clip", "tm", None),
        P(),
        P(None, None, "clip"),
        P(None, None, "clip"),
        P(None, None, "clip"),
        P(None, "clip"),
        P(None, "clip"),
        P(None, "clip"),
        P(None, "clip", None),
        P(None, "clip", None),
        P(None, "clip", None),
    )
    return jax.shard_map(shards, mesh=mesh, in_specs=in_specs, out_specs=out_specs, check_vma=False)
```

profile of v0, /device:TPU:0, one launch (start us, length us, event | category | flops | bytes accessed | tf_op | source)
XLA Modules:
  0.0 310.3 jit_solution(5738353770341371367)
XLA Ops:
  7.2 1.8 convert_element_type.54
  9.8 2.8 convert_multiply_fusion.1
  12.7 1.3 collective-permute-start.1
  14.0 3.0 collective-permute-start
  17.8 0.9 convert_element_type.64
  19.6 33.2 %all_gather.11 = bf16[256,512]{0,1:T(8,128)(2,1)S(1)} all-gather(bf16[256,64]{0,1:T(8,128)(2,1)S(1)} %convert_element_type.66), channel_id=1, replica_groups=mesh['clip'=8,'tm'=4] {'clip'}, dimensions={1}, use_global_device_ids=true | all-gather | bytes 294912 | tf_op jit(solution)/shard_map/all_gather | solution.py:74
  52.9 33.2 %all_gather.10 = bf16[3,512,256]{1,2,0:T(8,128)(2,1)S(1)} all-gather(bf16[3,512,32]{1,2,0:T(8,128)(2,1)S(1)} %convert_element_type.64), channel_id=1, replica_groups=mesh['clip'=8,'tm'=4] {'clip'}, dimensions={2}, use_global_device_ids=true | all-gather | bytes 884736 | tf_op jit(solution)/shard_map/all_gather | solution.py:73
  88.0 1.4 convolution_add_fusion.1
  89.4 1.7 slice_bitcast_fusion.3
  91.1 2.6 gather_fusion.1
  93.7 2.6 gather_fusion
  96.2 2.6 gather_fusion.3
  98.8 1.9 gather_fusion.2
  100.8 3.3 %fusion.12 = (f32[2,256,256]{2,1,0:T(8,128)S(1)}, f32[2,256,256]{2,1,0:T(8,128)S(1)}, f32[2,256,256]{2,1,0:T(8,128)}, f32[2,256,256]{2,1,0:T(8,128)}, f32[2,256,...) fusion(f32[2,256,512]{2,1,0:T(8,128)S(1)} %copy-done, ...), kind=kLoop, calls=%fused_computation.50 | loop fusion | flops 3932160 | bytes 7346176 | tf_op jit(solution)/shard_map/add | solution.py:104
  104.4 1.3 convolution_bitcast_fusion
  106.1 4.2 %scatter_custom_fusion.3 = f32[1024,256]{1,0:T(8,128)S(1)} fusion(s32[512]{0:T(512)S(1)} %bitcast.135, f32[512,256]{1,0:T(8,128)} %bitcast.127, f32[]{:T(128)} %constant.35.clone.1), kind=kCustom, calls=%fused_computation.74 | custom fusion | flops 131072 | bytes 1049088 | tf_op jit(solution)/shard_map/scatter-add | solution.py:107
  110.4 4.8 %scatter_custom_fusion.2 = f32[1024,256]{1,0:T(8,128)} fusion(s32[512]{0:T(512)S(1)} %bitcast.134, f32[512,256]{1,0:T(8,128)} %bitcast.126, f32[]{:T(128)} %constant.35.clone.1), kind=kCustom, calls=%fused_computation.76 | custom fusion | flops 131072 | bytes 1049088 | tf_op jit(solution)/shard_map/scatter-add | solution.py:107
  115.1 4.8 %scatter_custom_fusion.1 = f32[1024,256]{1,0:T(8,128)} fusion(s32[512]{0:T(512)S(1)} %bitcast.133, f32[512,256]{1,0:T(8,128)} %bitcast.125, f32[]{:T(128)} %constant.35.clone.1), kind=kCustom, calls=%fused_computation.78 | custom fusion | flops 131072 | bytes 1049088 | tf_op jit(solution)/shard_map/scatter-add | solution.py:107
  119.9 4.8 %scatter_custom_fusion = f32[1024,256]{1,0:T(8,128)} fusion(s32[512]{0:T(512)S(1)} %bitcast.132, f32[512,256]{1,0:T(8,128)} %bitcast.124, f32[]{:T(128)} %constant.35.clone.1), kind=kCustom, calls=%fused_computation.80 | custom fusion | flops 131072 | bytes 1049088 | tf_op jit(solution)/shard_map/scatter-add | solution.py:107
  125.4 1.3 pad_maximum_fusion.1
  126.8 2.3 pad_maximum_fusion
  130.0 1.4 collective-permute-start.3
  131.4 1.5 collective-permute-start.2
  134.5 1.4 collective-permute-done.2
  136.0 1.6 fusion.3
  137.6 149.0 %all-reduce.3.cloned.1.call-done = (f32[3,512,256]{1,2,0:T(8,128)}, f32[256,512]{0,1:T(8,128)}, f32[4,1024,256]{2,1,0:T(8,128)}) async-done(((f32[3,512,256]{1,2,0:T(8,128)}, f32[256,512]{0,1:T(8,128)}, f32[4,1024,256]{2,1,0:T(8,128)}), (f32[3,512,256]{1,2,0:T(8,128)}, f32[256,512]{0,1:T(8,128)}, f32[4,1024,256]{2,1,0:T(8,128)})) %all-reduce.3.cloned.1.call-update) | async-done | bytes 6291472 | tf_op jit(solution)/shard_map/psum | solution.py:144
  286.6 2.4 multiply_reduce_fusion.1
  289.0 1.8 multiply_reduce_fusion.2
  290.8 3.9 %multiply_reduce_fusion = f32[]{:T(128)} fusion(f32[4,1024,256]{2,1,0:T(8,128)} %get-tuple-element.39), kind=kLoop, calls=%fused_computation.9 | loop fusion | flops 2097151 | bytes 4194308 | tf_op jit(solution)/shard_map/reduce_sum | solution.py:145
  296.7 1.8 multiply_subtract_fusion.1
  298.5 1.5 multiply_subtract_fusion.2
  300.1 2.3 multiply_subtract_fusion
  (93 shorter events, 7.4 us)
Async XLA Ops:
  7.2 45.6 %copy-start.26 = (s32[2]{0:T(128)S(1)}, s32[2]{0:T(128)}, u32[]{:S(2)}) copy-start(s32[2]{0:T(128)} %param.18) | copy-start | bytes 28
  7.2 45.7 %copy-start.23 = (s32[4,2,256]{2,1,0:T(2,128)S(1)}, s32[4,2,256]{2,1,0:T(2,128)}, u32[]{:S(2)}) copy-start(s32[4,2,256]{2,1,0:T(2,128)} %param.19) | copy-start | bytes 24580
  7.2 82.2 %all-gather.2.cloned.1.call-start = ((), (), s32[]{:S(2)}) async-start(), calls=%async_computation | async-start | bytes 2359296 | tf_op jit(solution)/shard_map/all_gather | solution.py:75
  9.0 277.5 %all-reduce.3.cloned.1.call-start = ((), (), s32[]{:S(2)}) async-start(), calls=%async_computation.1 | async-start | bytes 12582912 | tf_op jit(solution)/shard_map/psum | solution.py:144
  9.8 78.2 %copy-start.11 = (bf16[2,256,512]{2,1,0:T(8,128)(2,1)S(1)}, bf16[2,256,512]{2,1,0:T(8,128)(2,1)}, u32[]{:S(2)}) copy-start(bf16[2,256,512]{2,1,0:T(8,128)(2,1)} %param.16) | copy-start | bytes 1572868
  12.7 73.8 %collective-permute-start.1 = (bf16[2,3,512]{2,1,0:T(4,128)(2,1)S(1)}, bf16[2,3,512]{2,1,0:T(4,128)(2,1)S(1)}, u32[]{:S(2)}, u32[]{:S(2)}) collective-permute-start(bf16[2,3,512]{2,1,0:T(4,128)(2,1)S(1)} %get-tuple-element.62), channel_id=1, source_target_pairs={{1,0},{2,1},{3,2},{5,4},{6,5},{7,6},{9,8},{10,9},{11,10},{13,12},{... | collective-permute-start | bytes 18440 | tf_op jit(solution)/shard_map/ppermute | solution.py:32
  14.0 72.9 %collective-permute-start = (bf16[2,3,512]{2,1,0:T(4,128)(2,1)S(1)}, bf16[2,3,512]{2,1,0:T(4,128)(2,1)S(1)}, u32[]{:S(2)}, u32[]{:S(2)}) collective-permute-start(bf16[2,3,512]{2,1,0:T(4,128)(2,1)S(1)} %get-tuple-element.61), channel_id=1, source_target_pairs={{0,1},{1,2},{2,3},{4,5},{5,6},{6,7},{8,9},{9,10},{10,11},{12,13},{... | collective-permute-start | bytes 18440 | tf_op jit(solution)/shard_map/ppermute | solution.py:30
  52.8 34.4 %copy-start.19 = (bf16[256,512]{0,1:T(8,128)(2,1)}, bf16[256,512]{0,1:T(8,128)(2,1)S(1)}, u32[]{:S(2)}) copy-start(bf16[256,512]{0,1:T(8,128)(2,1)S(1)} %all_gather.11) | copy-start | bytes 786436
  96.2 4.5 %copy-start = (f32[2,256,512]{2,1,0:T(8,128)S(1)}, f32[2,256,512]{2,1,0:T(8,128)}, u32[]{:S(2)}) copy-start(f32[2,256,512]{2,1,0:T(8,128)} %get-tuple-element.77) | copy-start | bytes 3145732
  100.8 3.3 %copy-start.17 = (f32[2,256,256]{2,1,0:T(8,128)S(1)}, f32[2,256,256]{2,1,0:T(8,128)}, u32[]{:S(2)}) copy-start(f32[2,256,256]{2,1,0:T(8,128)} %copy-done.16) | copy-start | bytes 1572868
  100.8 3.3 %copy-start.20 = (bf16[256,512]{0,1:T(8,128)(2,1)S(1)}, bf16[256,512]{0,1:T(8,128)(2,1)}, u32[]{:S(2)}) copy-start(bf16[256,512]{0,1:T(8,128)(2,1)} %copy-done.19) | copy-start | bytes 786436
  104.1 2.0 copy-start.7
  104.1 2.0 copy-start.9
  124.7 2.0 copy-start.1
  124.7 2.0 copy-start.2
  124.7 2.0 copy-start.3
  129.0 4.2 %copy-start.5 = (f32[2,256,256]{2,1,0:T(8,128)S(1)}, f32[2,256,256]{2,1,0:T(8,128)}, u32[]{:S(2)}) copy-start(f32[2,256,256]{2,1,0:T(8,128)} %get-tuple-element.59) | copy-start | bytes 1572868
  129.1 4.2 %copy-start.6 = (f32[2,256,256]{2,1,0:T(8,128)S(1)}, f32[2,256,256]{2,1,0:T(8,128)}, u32[]{:S(2)}) copy-start(f32[2,256,256]{2,1,0:T(8,128)} %get-tuple-element.60) | copy-start | bytes 1572868
  129.1 6.9 %copy-start.8 = (f32[2,256,256]{2,1,0:T(8,128)S(1)}, f32[2,256,256]{2,1,0:T(8,128)}, u32[]{:S(2)}) copy-start(f32[2,256,256]{2,1,0:T(8,128)} %copy-done.7) | copy-start | bytes 1572868
  129.1 6.9 %copy-start.10 = (f32[2,256,256]{2,1,0:T(8,128)S(1)}, f32[2,256,256]{2,1,0:T(8,128)}, u32[]{:S(2)}) copy-start(f32[2,256,256]{2,1,0:T(8,128)} %copy-done.9) | copy-start | bytes 1572868
  130.0 6.0 %copy-start.12 = (bf16[2,256,512]{2,1,0:T(8,128)(2,1)S(1)}, bf16[2,256,512]{2,1,0:T(8,128)(2,1)}, u32[]{:S(2)}) copy-start(bf16[2,256,512]{2,1,0:T(8,128)(2,1)} %param.16) | copy-start | bytes 1572868
  130.0 4.2 %collective-permute-start.3 = (bf16[2,3,256]{2,1,0:T(4,128)(2,1)S(1)}, bf16[2,3,256]{2,1,0:T(4,128)(2,1)S(1)}, u32[]{:S(2)}, u32[]{:S(2)}) collective-permute-start(bf16[2,3,256]{2,1,0:T(4,128)(2,1)S(1)} %get-tuple-element.64), channel_id=1, source_target_pairs={{0,1},{1,2},{2,3},{4,5},{5,6},{6,7},{8,9},{9,10},{10,11},{12,13},{... | collective-permute-start | bytes 9224 | tf_op jit(solution)/shard_map/ppermute | solution.py:30
  131.4 4.5 %collective-permute-start.2 = (bf16[2,3,256]{2,1,0:T(4,128)(2,1)S(1)}, bf16[2,3,256]{2,1,0:T(4,128)(2,1)S(1)}, u32[]{:S(2)}, u32[]{:S(2)}) collective-permute-start(bf16[2,3,256]{2,1,0:T(4,128)(2,1)S(1)} %get-tuple-element.63), channel_id=1, source_target_pairs={{1,0},{2,1},{3,2},{5,4},{6,5},{7,6},{9,8},{10,9},{11,10},{13,12},{... | collective-permute-start | bytes 9224 | tf_op jit(solution)/shard_map/ppermute | solution.py:32
  137.5 159.1 %copy-start.13 = (f32[3,512,32]{1,2,0:T(8,128)S(1)}, f32[3,512,32]{1,2,0:T(8,128)}, u32[]{:S(2)}) copy-start(f32[3,512,32]{1,2,0:T(8,128)} %param.21) | copy-start | bytes 589828
  137.5 159.2 %copy-start.21 = (f32[3,512,32]{1,2,0:T(8,128)S(1)}, f32[3,512,32]{1,2,0:T(8,128)}, u32[]{:S(2)}) copy-start(f32[3,512,32]{1,2,0:T(8,128)} %param.24) | copy-start | bytes 589828
  137.5 159.2 %copy-start.22 = (f32[3,512,32]{1,2,0:T(8,128)S(1)}, f32[3,512,32]{1,2,0:T(8,128)}, u32[]{:S(2)}) copy-start(f32[3,512,32]{1,2,0:T(8,128)} %param.25) | copy-start | bytes 589828
  137.5 161.0 %copy-start.18 = (f32[256,64]{0,1:T(8,128)S(1)}, f32[256,64]{0,1:T(8,128)}, u32[]{:S(2)}) copy-start(f32[256,64]{0,1:T(8,128)} %param.22) | copy-start | bytes 196612
  137.5 161.0 %copy-start.24 = (f32[256,64]{0,1:T(8,128)S(1)}, f32[256,64]{0,1:T(8,128)}, u32[]{:S(2)}) copy-start(f32[256,64]{0,1:T(8,128)} %param.26) | copy-start | bytes 196612
  137.5 161.0 %copy-start.25 = (f32[256,64]{0,1:T(8,128)S(1)}, f32[256,64]{0,1:T(8,128)}, u32[]{:S(2)}) copy-start(f32[256,64]{0,1:T(8,128)} %param.27) | copy-start | bytes 196612
  137.6 162.5 %copy-start.4 = (f32[4,128,256]{2,1,0:T(8,128)S(1)}, f32[4,128,256]{2,1,0:T(8,128)}, u32[]{:S(2)}) copy-start(f32[4,128,256]{2,1,0:T(8,128)} %param.23) | copy-start | bytes 1572868
  137.6 162.5 %copy-start.14 = (f32[4,128,256]{2,1,0:T(8,128)S(1)}, f32[4,128,256]{2,1,0:T(8,128)}, u32[]{:S(2)}) copy-start(f32[4,128,256]{2,1,0:T(8,128)} %param.28) | copy-start | bytes 1572868
  137.6 162.5 %copy-start.15 = (f32[4,128,256]{2,1,0:T(8,128)S(1)}, f32[4,128,256]{2,1,0:T(8,128)}, u32[]{:S(2)}) copy-start(f32[4,128,256]{2,1,0:T(8,128)} %param.29) | copy-start | bytes 1572868
  (1 other events, 0.8 us)
Sparse Core Ops, SparseCore 0:
  10.8 58.7 all-gather.1
  129.2 157.3 all-reduce.2
where the time goes:
time: 311 us; the launch traced here: 310 us
  waiting for transfers between devices  150 us (48%)
  blocking collectives  66.4 us (21%)
  other arithmetic  48.1 us (15%)
  between operations  18.6 us (6%)
  local copies, waits for them, and re-layouts  12.2 us (4%)
  starting transfers between devices  7.34 us (2%)
  matrix products  7.32 us (2%)
    psum x1, waiting for transfers between devices, shards(): lax.psum((local_grads[0], local_grads[1], local_grads[2]), ('clip', 'tm'))  149 us
    all_gather x1, blocking collectives, shards(): lax.all_gather(pointwise_conv.astype(jnp.bfloat16), 'clip', axis=1, tiled...  33.2 us
    all_gather x1, blocking collectives, shards(): lax.all_gather(dilated_kernel_weight.astype(jnp.bfloat16), 'clip', axis=2...  33.2 us
    scatter-add x4, other arithmetic, shards(): jax.ops.segment_sum(code_grad.reshape(-1, DG), code_ids[slot].reshape(-1)...  18.6 us
    gather x4, local copies, waits for them, and re-layouts, shards(): jnp.take(table_full[slot], code_ids[slot], axis=0).astype(jnp.float32)  9.65 us
    reduce_sum x3, other arithmetic, shards(): squared = sum((jnp.sum(piece * piece) for piece in whole))  8.06 us
  transfers between devices with their start and end apart: 6, of which 2 were waited for; matrix products, arithmetic and copies ran while one was open for 4% of the time, Pallas kernels for 0%

commit v1 on v0

--- a/solution.py
+++ b/solution.py
@@ -67,6 +67,14 @@
     codebook_first,
     codebook_second,
 ):
+
+    def edit_terms(target):
+        bus_axis = "clip"
+        shard_axis = "tm"
+        for j0 in (shard_axis, bus_axis):
+            target = lax.psum(target, axis_name=j0)
+        return target
+
     clip_rank = lax.axis_index("clip")
     time_rank = lax.axis_index("tm")
     dilated_full, pointwise_full, table_full = (
@@ -141,7 +149,7 @@
     dilated_grad = jnp.stack(dilated_parts, axis=0)
     features_gradient = frame_mask * (latent_grad + elu_slope(start) * act_grad)
     local_grads = (dilated_grad, pointwise_grad, table_grad)
-    whole = lax.psum((local_grads[0], local_grads[1], local_grads[2]), ("clip", "tm"))
+    whole = edit_terms((local_grads[0], local_grads[1], local_grads[2]))
     squared = sum((jnp.sum(piece * piece) for piece in whole))
     shares = (
         lax.dynamic_slice_in_dim(

time: 311 us -> 493 us (1.59)
  waiting for transfers between devices: 150 us -> 332 us
    psum x1 -> x2, waiting for transfers between devices: 149 us -> 331 us  [edit_terms(): target = lax.psum(target, axis_name=j0)]
  transfers between devices with their start and end apart: 6 -> 7, of which waited for: 2 -> 3; matrix products, arithmetic and copies ran while one was open for 4% -> 2% of each run, Pallas kernels for 0% -> 0%
where the time goes in v1:
time: 493 us; the launch traced here: 492 us
  waiting for transfers between devices  332 us (67%)
  blocking collectives  66.4 us (13%)
  other arithmetic  48 us (10%)
  between operations  18.2 us (4%)
  local copies, waits for them, and re-layouts  12.3 us (2%)
  starting transfers between devices  7.61 us (2%)
  matrix products  7.33 us (1%)
    psum x2, waiting for transfers between devices, edit_terms(): target = lax.psum(target, axis_name=j0)  331 us
    all_gather x1, blocking collectives, shards(): lax.all_gather(pointwise_conv.astype(jnp.bfloat16), 'clip', axis=1, tiled...  33.2 us
    all_gather x1, blocking collectives, shards(): lax.all_gather(dilated_kernel_weight.astype(jnp.bfloat16), 'clip', axis=2...  33.2 us
    scatter-add x4, other arithmetic, shards(): jax.ops.segment_sum(code_grad.reshape(-1, DG), code_ids[slot].reshape(-1)...  18.6 us
  transfers between devices with their start and end apart: 7, of which 3 were waited for; matrix products, arithmetic and copies ran while one was open for 2% of the time, Pallas kernels for 0%

profile of v1, /device:TPU:0, one launch (start us, length us, event | category | flops | bytes accessed | tf_op | source)
XLA Modules:
  0.0 491.8 jit_solution(14045445107942005590)
XLA Ops:
  7.2 1.8 convert_element_type.54
  9.8 2.8 convert_multiply_fusion.1
  12.7 1.3 collective-permute-start.1
  14.0 3.0 collective-permute-start
  17.8 0.9 convert_element_type.64
  19.6 33.2 %all_gather.11 = bf16[256,512]{0,1:T(8,128)(2,1)S(1)} all-gather(bf16[256,64]{0,1:T(8,128)(2,1)S(1)} %convert_element_type.66), channel_id=1, replica_groups=mesh['clip'=8,'tm'=4] {'clip'}, dimensions={1}, use_global_device_ids=true | all-gather | bytes 294912 | tf_op jit(solution)/shard_map/all_gather | solution.py:82
  52.9 33.2 %all_gather.10 = bf16[3,512,256]{1,2,0:T(8,128)(2,1)S(1)} all-gather(bf16[3,512,32]{1,2,0:T(8,128)(2,1)S(1)} %convert_element_type.64), channel_id=1, replica_groups=mesh['clip'=8,'tm'=4] {'clip'}, dimensions={2}, use_global_device_ids=true | all-gather | bytes 884736 | tf_op jit(solution)/shard_map/all_gather | solution.py:81
  88.0 1.4 convolution_add_fusion.1
  89.5 1.7 slice_bitcast_fusion.3
  91.1 2.6 gather_fusion.1
  93.7 2.6 gather_fusion
  96.2 2.6 gather_fusion.3
  98.8 1.9 gather_fusion.2
  100.8 3.3 fusion.12
  104.4 1.3 convolution_bitcast_fusion
  106.1 4.2 scatter_custom_fusion.3
  110.4 4.8 scatter_custom_fusion.2
  115.1 4.8 scatter_custom_fusion.1
  120.0 4.8 scatter_custom_fusion
  125.4 1.3 pad_maximum_fusion.1
  126.8 2.3 pad_maximum_fusion
  129.1 120.9 %all-reduce.7.cloned.1.call-done = (f32[3,512,256]{1,2,0:T(8,128)}, f32[256,512]{0,1:T(8,128)}, f32[4,1024,256]{2,1,0:T(8,128)}) async-done(((f32[3,512,256]{1,2,0:T(8,128)}, f32[256,512]{0,1:T(8,128)}, f32[4,1024,256]{2,1,0:T(8,128)}), (f32[3,512,256]{1,2,0:T(8,128)}, f32[256,512]{0,1:T(8,128)}, f32[4,1024,256]{2,1,0:T(8,128)})) %all-reduce.7.cloned.1.call-update) | async-done | bytes 6291472 | tf_op jit(solution)/shard_map/psum | solution.py:75
  250.9 1.7 collective-permute-start.3
  252.6 1.5 collective-permute-start.2
  256.2 1.6 fusion.3
  257.8 210.5 %all-reduce.5.cloned.1.call-done = (f32[3,512,256]{1,2,0:T(8,128)}, f32[256,512]{0,1:T(8,128)}, f32[4,1024,256]{2,1,0:T(8,128)}) async-done(((f32[3,512,256]{1,2,0:T(8,128)}, f32[256,512]{0,1:T(8,128)}, f32[4,1024,256]{2,1,0:T(8,128)}), (f32[3,512,256]{1,2,0:T(8,128)}, f32[256,512]{0,1:T(8,128)}, f32[4,1024,256]{2,1,0:T(8,128)})) %all-reduce.5.cloned.1.call-update) | async-done | bytes 6291472 | tf_op jit(solution)/shard_map/psum | solution.py:75
  468.3 2.4 multiply_reduce_fusion.1
  470.7 1.8 multiply_reduce_fusion.2
  472.5 3.9 multiply_reduce_fusion
  478.4 1.8 multiply_subtract_fusion.1
  480.3 1.5 multiply_subtract_fusion.2
  481.8 2.3 multiply_subtract_fusion
  (96 shorter events, 8.0 us)
Async XLA Ops:
  7.2 45.6 %copy-start.26 = (s32[2]{0:T(128)S(1)}, s32[2]{0:T(128)}, u32[]{:S(2)}) copy-start(s32[2]{0:T(128)} %param.18) | copy-start | bytes 28
  7.2 45.7 %copy-start.23 = (s32[4,2,256]{2,1,0:T(2,128)S(1)}, s32[4,2,256]{2,1,0:T(2,128)}, u32[]{:S(2)}) copy-start(s32[4,2,256]{2,1,0:T(2,128)} %param.19) | copy-start | bytes 24580
  7.2 82.3 %all-gather.2.cloned.1.call-start = ((), (), s32[]{:S(2)}) async-start(), calls=%async_computation | async-start | bytes 2359296 | tf_op jit(solution)/shard_map/all_gather | solution.py:83
  9.0 241.0 %all-reduce.7.cloned.1.call-start = ((), (), s32[]{:S(2)}) async-start(), calls=%async_computation.2 | async-start | bytes 12582912 | tf_op jit(solution)/shard_map/psum | solution.py:75
  9.8 78.2 %copy-start.11 = (bf16[2,256,512]{2,1,0:T(8,128)(2,1)S(1)}, bf16[2,256,512]{2,1,0:T(8,128)(2,1)}, u32[]{:S(2)}) copy-start(bf16[2,256,512]{2,1,0:T(8,128)(2,1)} %param.16) | copy-start | bytes 1572868
  12.7 73.8 %collective-permute-start.1 = (bf16[2,3,512]{2,1,0:T(4,128)(2,1)S(1)}, bf16[2,3,512]{2,1,0:T(4,128)(2,1)S(1)}, u32[]{:S(2)}, u32[]{:S(2)}) collective-permute-start(bf16[2,3,512]{2,1,0:T(4,128)(2,1)S(1)} %get-tuple-element.65), channel_id=1, source_target_pairs={{1,0},{2,1},{3,2},{5,4},{6,5},{7,6},{9,8},{10,9},{11,10},{13,12},{... | collective-permute-start | bytes 18440 | tf_op jit(solution)/shard_map/ppermute | solution.py:32
  14.0 72.9 %collective-permute-start = (bf16[2,3,512]{2,1,0:T(4,128)(2,1)S(1)}, bf16[2,3,512]{2,1,0:T(4,128)(2,1)S(1)}, u32[]{:S(2)}, u32[]{:S(2)}) collective-permute-start(bf16[2,3,512]{2,1,0:T(4,128)(2,1)S(1)} %get-tuple-element.64), channel_id=1, source_target_pairs={{0,1},{1,2},{2,3},{4,5},{5,6},{6,7},{8,9},{9,10},{10,11},{12,13},{... | collective-permute-start | bytes 18440 | tf_op jit(solution)/shard_map/ppermute | solution.py:30
  52.8 34.4 %copy-start.19 = (bf16[256,512]{0,1:T(8,128)(2,1)}, bf16[256,512]{0,1:T(8,128)(2,1)S(1)}, u32[]{:S(2)}) copy-start(bf16[256,512]{0,1:T(8,128)(2,1)S(1)} %all_gather.11) | copy-start | bytes 786436
  96.2 4.5 copy-start
  100.8 3.3 copy-start.17
  100.8 3.3 copy-start.20
  104.1 2.0 copy-start.7
  104.1 2.0 copy-start.9
  124.7 2.0 copy-start.2
  124.7 2.0 copy-start.3
  129.1 125.3 %copy-start.5 = (f32[2,256,256]{2,1,0:T(8,128)S(1)}, f32[2,256,256]{2,1,0:T(8,128)}, u32[]{:S(2)}) copy-start(f32[2,256,256]{2,1,0:T(8,128)} %get-tuple-element.62) | copy-start | bytes 1572868
  129.1 125.3 %copy-start.6 = (f32[2,256,256]{2,1,0:T(8,128)S(1)}, f32[2,256,256]{2,1,0:T(8,128)}, u32[]{:S(2)}) copy-start(f32[2,256,256]{2,1,0:T(8,128)} %get-tuple-element.63) | copy-start | bytes 1572868
  129.1 339.2 %all-reduce.5.cloned.1.call-start = ((), (), s32[]{:S(2)}) async-start(), calls=%async_computation.1 | async-start | bytes 12582912 | tf_op jit(solution)/shard_map/psum | solution.py:75
  250.0 6.1 %copy-start.8 = (f32[2,256,256]{2,1,0:T(8,128)S(1)}, f32[2,256,256]{2,1,0:T(8,128)}, u32[]{:S(2)}) copy-start(f32[2,256,256]{2,1,0:T(8,128)} %copy-done.7) | copy-start | bytes 1572868
  250.0 6.1 %copy-start.10 = (f32[2,256,256]{2,1,0:T(8,128)S(1)}, f32[2,256,256]{2,1,0:T(8,128)}, u32[]{:S(2)}) copy-start(f32[2,256,256]{2,1,0:T(8,128)} %copy-done.9) | copy-start | bytes 1572868
  250.9 5.3 %copy-start.12 = (bf16[2,256,512]{2,1,0:T(8,128)(2,1)S(1)}, bf16[2,256,512]{2,1,0:T(8,128)(2,1)}, u32[]{:S(2)}) copy-start(bf16[2,256,512]{2,1,0:T(8,128)(2,1)} %param.16) | copy-start | bytes 1572868
  250.9 4.4 collective-permute-start.3
  252.6 3.6 collective-permute-start.2
  257.7 220.7 %copy-start.13 = (f32[3,512,32]{1,2,0:T(8,128)S(1)}, f32[3,512,32]{1,2,0:T(8,128)}, u32[]{:S(2)}) copy-start(f32[3,512,32]{1,2,0:T(8,128)} %param.21) | copy-start | bytes 589828
  257.7 220.7 %copy-start.21 = (f32[3,512,32]{1,2,0:T(8,128)S(1)}, f32[3,512,32]{1,2,0:T(8,128)}, u32[]{:S(2)}) copy-start(f32[3,512,32]{1,2,0:T(8,128)} %param.24) | copy-start | bytes 589828
  257.7 220.7 %copy-start.22 = (f32[3,512,32]{1,2,0:T(8,128)S(1)}, f32[3,512,32]{1,2,0:T(8,128)}, u32[]{:S(2)}) copy-start(f32[3,512,32]{1,2,0:T(8,128)} %param.25) | copy-start | bytes 589828
  257.7 222.5 %copy-start.18 = (f32[256,64]{0,1:T(8,128)S(1)}, f32[256,64]{0,1:T(8,128)}, u32[]{:S(2)}) copy-start(f32[256,64]{0,1:T(8,128)} %param.22) | copy-start | bytes 196612
  257.7 222.5 %copy-start.24 = (f32[256,64]{0,1:T(8,128)S(1)}, f32[256,64]{0,1:T(8,128)}, u32[]{:S(2)}) copy-start(f32[256,64]{0,1:T(8,128)} %param.26) | copy-start | bytes 196612
  257.7 222.5 %copy-start.25 = (f32[256,64]{0,1:T(8,128)S(1)}, f32[256,64]{0,1:T(8,128)}, u32[]{:S(2)}) copy-start(f32[256,64]{0,1:T(8,128)} %param.27) | copy-start | bytes 196612
  257.8 224.0 %copy-start.4 = (f32[4,128,256]{2,1,0:T(8,128)S(1)}, f32[4,128,256]{2,1,0:T(8,128)}, u32[]{:S(2)}) copy-start(f32[4,128,256]{2,1,0:T(8,128)} %param.23) | copy-start | bytes 1572868
  257.8 224.0 %copy-start.14 = (f32[4,128,256]{2,1,0:T(8,128)S(1)}, f32[4,128,256]{2,1,0:T(8,128)}, u32[]{:S(2)}) copy-start(f32[4,128,256]{2,1,0:T(8,128)} %param.28) | copy-start | bytes 1572868
  257.8 224.0 %copy-start.15 = (f32[4,128,256]{2,1,0:T(8,128)S(1)}, f32[4,128,256]{2,1,0:T(8,128)}, u32[]{:S(2)}) copy-start(f32[4,128,256]{2,1,0:T(8,128)} %param.29) | copy-start | bytes 1572868
  (2 other events, 2.8 us)
Sparse Core Ops, SparseCore 0:
  10.8 58.7 all-gather.1
  129.2 120.7 all-reduce.6
  254.3 213.9 all-reduce.4
